TPU v7x, 128 devices: a whole 4x4x4 slice. The times are simulated.
128 devices in a mesh: prow: 16 (over x, z), pcol: 8 (over y, core).
Axes of the slice: x: 4, y: 4, z: 4, core: 2. Of those that a mesh axis runs over, the one named last changes fastest.
Arguments:
- rhs: float32 [31, 64, 2048], P(None, None, 'prow'), may hold values from -6 to 6
- factor: bfloat16 [98, 2048, 2048], P(None, 'prow', 'pcol'), may hold values from -0.03125 to 0.03125
- inverse: bfloat16 [31, 2048, 2048], P(None, 'pcol', 'prow')
- pattern: int32 [98], replicated, may hold values 0 or 1
Outputs:
- solution: float32 [31, 64, 2048], P(None, None, 'prow')
- forward_solution: float32 [31, 64, 2048], P(None, None, 'pcol')
All inputs are finite; a program needn't handle non-finite values.
Results may differ from a plain program's by a relative error of at most 0.011.
Values sent between devices are 32-bit elements; how exact they have to be, the bound alone decides.
No kernel may reach another device: no remote copies, remote signals or barrier semaphores. Data moves between devices by JAX's collectives and lax.ppermute only.
A program may use at most 64 MiB of HBM per device.

v0:
```python
import jax
import jax.numpy as jnp
from jax import lax
from jax.sharding import PartitionSpec as P

LEV = 5


def block_start(tree_depth):
    return (tree_depth - 2) * 2**tree_depth + 2


def sum_columns(values):
    result = lax.psum(values, "pcol")
    return lax.optimization_barrier(result)


def sum_rows(values):
    result = lax.psum(values, "prow")
    return lax.optimization_barrier(result)


def per_device(rhs, factor, inverse, pattern):
    live = pattern.astype(jnp.float32)
    partial_value = jnp.zeros(rhs.shape, jnp.float32)
    forward_levels = [None] * LEV
    for tree_depth in range(LEV - 1, -1, -1):
        first = 2**tree_depth - 1
        count = 2**tree_depth
        residual = rhs[first : first + count]
        if tree_depth < LEV - 1:
            residual = residual - sum_columns(partial_value[first : first + count])
        rounded = residual.astype(jnp.bfloat16)
        pieces = jnp.einsum(
            "nrc,nwc->nrw",
            rounded,
            inverse[first : first + count],
            preferred_element_type=jnp.float32,
        )
        forward = sum_rows(pieces)
        forward_levels[tree_depth] = forward
        narrow = forward.astype(jnp.bfloat16)
        if tree_depth > 0:
            start = block_start(tree_depth)
            weights = live[start : start + count * tree_depth].reshape(count, tree_depth)
            for upward in range(1, tree_depth + 1):
                blocks = factor[start + upward - 1 : start + count * tree_depth : tree_depth]
                terms = jnp.einsum(
                    "nrc,nwc->nrw", narrow, blocks, preferred_element_type=jnp.float32
                )
                terms = terms * weights[:, upward - 1][:, None, None]
                groups = count >> upward
                terms = terms.reshape((groups, 2**upward) + terms.shape[1:]).sum(axis=1)
                target = 2 ** (tree_depth - upward) - 1
                partial_value = partial_value.at[target : target + groups].add(terms)
    solved = [None] * LEV
    solved_narrow = [None] * LEV
    for tree_depth in range(LEV):
        first = 2**tree_depth - 1
        count = 2**tree_depth
        target_vec = forward_levels[tree_depth]
        if tree_depth > 0:
            start = block_start(tree_depth)
            weights = live[start : start + count * tree_depth].reshape(count, tree_depth)
            gathered = jnp.zeros(target_vec.shape, jnp.float32)
            for upward in range(1, tree_depth + 1):
                blocks = factor[start + upward - 1 : start + count * tree_depth : tree_depth]
                above = jnp.repeat(solved_narrow[tree_depth - upward], 2**upward, axis=0)
                terms = jnp.einsum(
                    "nrw,nwc->nrc", above, blocks, preferred_element_type=jnp.float32
                )
                gathered = gathered + terms * weights[:, upward - 1][:, None, None]
            target_vec = target_vec - sum_rows(gathered)
        rounded = target_vec.astype(jnp.bfloat16)
        pieces = jnp.einsum(
            "nrw,nwc->nrc",
            rounded,
            inverse[first : first + count],
            preferred_element_type=jnp.float32,
        )
        solution = sum_columns(pieces)
        solved[tree_depth] = solution
        solved_narrow[tree_depth] = solution.astype(jnp.bfloat16)
    return (jnp.concatenate(solved, axis=0), jnp.concatenate(forward_levels, axis=0))


def solution(mesh):
    in_specs = (P(None, None, "prow"), P(None, "prow", "pcol"), P(None, "pcol", "prow"), P())
    out_specs = (P(None, None, "prow"), P(None, None, "pcol"))
    return jax.shard_map(
        per_device, mesh=mesh, in_specs=in_specs, out_specs=out_specs, check_vma=False
    )
```

profile of v0, /device:TPU:0, one launch (start us, length us, event | category | flops | bytes accessed | tf_op | source)
XLA Modules:
  0.0 1293.9 jit_solution(4972876091253898043)
XLA Ops:
  7.2 2.8 fusion.20
  10.3 0.2 slice_reduce_fusion
  10.5 90.9 %all-reduce.18.cloned.1.call-done = f32[16,64,256]{2,1,0:T(8,128)} async-done(((f32[16,64,256]{2,1,0:T(8,128)}), f32[16,64,256]{2,1,0:T(8,128)}) %all-reduce.18.cloned.1.call-update) | async-done | bytes 1048592 | tf_op jit(solution)/shard_map/psum | solution.py:19
  101.5 1.3 convert_element_type.57
  102.8 1.7 bitcast_reduce_fusion.2
  104.5 1.7 bitcast_reduce_fusion.1
  106.2 1.7 bitcast_reduce_fusion
  107.9 1.7 fusion.5
  109.8 0.7 slice.423
  110.6 59.1 %all-reduce.20.cloned.1.call-done = f32[8,64,128]{2,1,0:T(8,128)} async-done(((f32[8,64,128]{2,1,0:T(8,128)}), f32[8,64,128]{2,1,0:T(8,128)}) %all-reduce.20.cloned.1.call-update) | async-done | bytes 262160 | tf_op jit(solution)/shard_map/psum | solution.py:14
  169.8 2.3 fusion.31
  172.5 85.8 %all-reduce.22.cloned.1.call-done = f32[8,64,256]{2,1,0:T(8,128)} async-done(((f32[8,64,256]{2,1,0:T(8,128)}), f32[8,64,256]{2,1,0:T(8,128)}) %all-reduce.22.cloned.1.call-update) | async-done | bytes 524304 | tf_op jit(solution)/shard_map/psum | solution.py:19
  258.3 1.6 bitcast_reduce_fusion.4
  260.0 1.5 bitcast_reduce_fusion.3
  261.6 0.7 slice.426
  262.3 58.7 %all-reduce.24.cloned.1.call-done = f32[4,64,128]{2,1,0:T(8,128)} async-done(((f32[4,64,128]{2,1,0:T(8,128)}), f32[4,64,128]{2,1,0:T(8,128)}) %all-reduce.24.cloned.1.call-update) | async-done | bytes 131088 | tf_op jit(solution)/shard_map/psum | solution.py:14
  321.0 2.0 fusion.45
  323.4 84.9 %all-reduce.26.cloned.1.call-done = f32[4,64,256]{2,1,0:T(8,128)} async-done(((f32[4,64,256]{2,1,0:T(8,128)}), f32[4,64,256]{2,1,0:T(8,128)}) %all-reduce.26.cloned.1.call-update) | async-done | bytes 262160 | tf_op jit(solution)/shard_map/psum | solution.py:19
  408.3 1.3 bitcast_reduce_fusion.5
  409.6 0.6 fusion.76
  410.3 1.3 fusion.7
  411.7 57.4 %all-reduce.28.cloned.1.call-done = f32[2,64,128]{2,1,0:T(8,128)} async-done(((f32[2,64,128]{2,1,0:T(8,128)}), f32[2,64,128]{2,1,0:T(8,128)}) %all-reduce.28.cloned.1.call-update) | async-done | bytes 65552 | tf_op jit(solution)/shard_map/psum | solution.py:14
  469.1 1.8 fusion.57
  470.9 1.2 fusion.8
  472.2 82.4 %all-reduce.30.cloned.1.call-done = f32[2,64,256]{2,1,0:T(8,128)} async-done(((f32[2,64,256]{2,1,0:T(8,128)}), f32[2,64,256]{2,1,0:T(8,128)}) %all-reduce.30.cloned.1.call-update) | async-done | bytes 131088 | tf_op jit(solution)/shard_map/psum | solution.py:19
  554.6 1.1 fusion.9
  555.7 24.1 %psum.133 = f32[1,64,128]{2,1,0:T(8,128)S(1)} all-reduce(f32[1,64,128]{2,1,0:T(8,128)S(1)} %fusion.71), channel_id=1, replica_groups=mesh['prow'=16,'pcol'=8] {'pcol'}, use_global_device_ids=true, to_apply=%region_17.0 | all-reduce | flops 8192 | bytes 65536 | tf_op jit(solution)/shard_map/psum | solution.py:14
  579.8 1.6 convolution_bitcast_fusion
  581.5 77.6 %all-reduce.32.cloned.1.call-done = f32[1,64,256]{2,1,0:T(8,128)} async-done(((f32[1,64,256]{2,1,0:T(8,128)}), f32[1,64,256]{2,1,0:T(8,128)}) %all-reduce.32.cloned.1.call-update) | async-done | bytes 65552 | tf_op jit(solution)/shard_map/psum | solution.py:19
  659.1 1.0 convolution_bitcast_fusion.1
  660.1 24.1 %psum.135 = f32[1,64,128]{2,1,0:T(8,128)S(1)} all-reduce(f32[1,64,128]{2,1,0:T(8,128)S(1)} %convolution_bitcast_fusion.1), channel_id=1, replica_groups=mesh['prow'=16,'pcol'=8] {'pcol'}, use_global_device_ids=true, to_apply=%region_19.0 | all-reduce | flops 8192 | bytes 65536 | tf_op jit(solution)/shard_map/psum | solution.py:14
  684.2 1.7 convolution_multiply_fusion.18
  686.0 79.1 %all-reduce.34.cloned.1.call-done = f32[2,64,256]{2,1,0:T(8,128)} async-done(((f32[2,64,256]{2,1,0:T(8,128)}), f32[2,64,256]{2,1,0:T(8,128)}) %all-reduce.34.cloned.1.call-update) | async-done | bytes 131088 | tf_op jit(solution)/shard_map/psum | solution.py:19
  765.1 1.8 fusion.55
  767.0 58.9 %all-reduce.36.cloned.1.call-done = f32[2,64,128]{2,1,0:T(8,128)} async-done(((f32[2,64,128]{2,1,0:T(8,128)}), f32[2,64,128]{2,1,0:T(8,128)}) %all-reduce.36.cloned.1.call-update) | async-done | bytes 65552 | tf_op jit(solution)/shard_map/psum | solution.py:14
  825.9 0.9 fusion.86
  826.9 1.1 convolution_multiply_fusion.12
  828.0 1.8 fusion.6
  829.9 83.5 %all-reduce.38.cloned.1.call-done = f32[4,64,256]{2,1,0:T(8,128)} async-done(((f32[4,64,256]{2,1,0:T(8,128)}), f32[4,64,256]{2,1,0:T(8,128)}) %all-reduce.38.cloned.1.call-update) | async-done | bytes 262160 | tf_op jit(solution)/shard_map/psum | solution.py:19
  913.4 1.9 fusion.43
  915.3 59.3 %all-reduce.40.cloned.1.call-done = f32[4,64,128]{2,1,0:T(8,128)} async-done(((f32[4,64,128]{2,1,0:T(8,128)}), f32[4,64,128]{2,1,0:T(8,128)}) %all-reduce.40.cloned.1.call-update) | async-done | bytes 131088 | tf_op jit(solution)/shard_map/psum | solution.py:14
  974.7 1.0 fusion.85
  975.7 1.3 convolution_multiply_fusion.10
  977.0 1.3 fusion.4
  978.3 2.1 fusion.3
  980.4 84.4 %all-reduce.42.cloned.1.call-done = f32[8,64,256]{2,1,0:T(8,128)} async-done(((f32[8,64,256]{2,1,0:T(8,128)}), f32[8,64,256]{2,1,0:T(8,128)}) %all-reduce.42.cloned.1.call-update) | async-done | bytes 524304 | tf_op jit(solution)/shard_map/psum | solution.py:19
  1064.9 2.1 fusion.29
  1067.0 59.7 %all-reduce.44.cloned.1.call-done = f32[8,64,128]{2,1,0:T(8,128)} async-done(((f32[8,64,128]{2,1,0:T(8,128)}), f32[8,64,128]{2,1,0:T(8,128)}) %all-reduce.44.cloned.1.call-update) | async-done | bytes 262160 | tf_op jit(solution)/shard_map/psum | solution.py:14
  1126.7 1.1 fusion.84
  1127.9 0.9 copy-done.5
  1128.8 1.6 convolution_multiply_fusion.3
  1130.4 1.6 fusion.2
  1132.1 1.5 fusion.1
  1133.6 2.5 fusion
  1136.2 0.6 constant_dynamic-update-slice_fusion.9
  1136.9 0.7 constant_dynamic-update-slice_fusion.8
  1137.5 0.7 constant_dynamic-update-slice_fusion.7
  1138.3 84.3 %all-reduce.46.cloned.1.call-done = f32[16,64,256]{2,1,0:T(8,128)} async-done(((f32[16,64,256]{2,1,0:T(8,128)}), f32[16,64,256]{2,1,0:T(8,128)}) %all-reduce.46.cloned.1.call-update) | async-done | bytes 1048592 | tf_op jit(solution)/shard_map/psum | solution.py:19
  1222.5 2.7 fusion.18
  1225.2 0.8 constant_dynamic-update-slice_fusion.6
  1226.1 1.1 constant_dynamic-update-slice_fusion.5
  1227.1 58.2 %all-reduce.48.cloned.1.call-done = f32[16,64,128]{2,1,0:T(8,128)} async-done(((f32[16,64,128]{2,1,0:T(8,128)}), f32[16,64,128]{2,1,0:T(8,128)}) %all-reduce.48.cloned.1.call-update) | async-done | bytes 524304 | tf_op jit(solution)/shard_map/psum | solution.py:14
  1285.3 1.1 constant_dynamic-update-slice_fusion
  1286.4 0.9 copy-done.7
  (72 shorter events, 2.3 us)
Async XLA Ops:
  7.2 3.0 copy-start.8
  7.2 94.3 %all-reduce.18.cloned.1.call-start = ((), (), s32[]{:S(2)}) async-start(), calls=%async_computation | async-start | bytes 2097152 | tf_op jit(solution)/shard_map/psum | solution.py:19
  10.1 159.7 %all-reduce.20.cloned.1.call-start = ((), (), s32[]{:S(2)}) async-start(), calls=%async_computation.1 | async-start | bytes 524288 | tf_op jit(solution)/shard_map/psum | solution.py:14
  110.6 147.7 %all-reduce.22.cloned.1.call-start = ((), (), s32[]{:S(2)}) async-start(), calls=%async_computation.2 | async-start | bytes 1048576 | tf_op jit(solution)/shard_map/psum | solution.py:19
  172.1 148.9 %all-reduce.24.cloned.1.call-start = ((), (), s32[]{:S(2)}) async-start(), calls=%async_computation.3 | async-start | bytes 262144 | tf_op jit(solution)/shard_map/psum | solution.py:14
  258.3 152.0 %copy-start = (f32[8,64,256]{2,1,0:T(8,128)S(1)}, f32[8,64,256]{2,1,0:T(8,128)}, u32[]{:S(2)}) copy-start(f32[8,64,256]{2,1,0:T(8,128)} %all-reduce.22.cloned.1.call-done) | copy-start | bytes 1572868
  262.2 146.0 %all-reduce.26.cloned.1.call-start = ((), (), s32[]{:S(2)}) async-start(), calls=%async_computation.4 | async-start | bytes 524288 | tf_op jit(solution)/shard_map/psum | solution.py:19
  323.0 146.1 %all-reduce.28.cloned.1.call-start = ((), (), s32[]{:S(2)}) async-start(), calls=%async_computation.5 | async-start | bytes 131072 | tf_op jit(solution)/shard_map/psum | solution.py:14
  408.3 505.1 %copy-start.2 = (f32[4,64,256]{2,1,0:T(8,128)S(1)}, f32[4,64,256]{2,1,0:T(8,128)}, u32[]{:S(2)}) copy-start(f32[4,64,256]{2,1,0:T(8,128)} %all-reduce.26.cloned.1.call-done) | copy-start | bytes 786436
  410.2 144.3 %all-reduce.30.cloned.1.call-start = ((), (), s32[]{:S(2)}) async-start(), calls=%async_computation.6 | async-start | bytes 262144 | tf_op jit(solution)/shard_map/psum | solution.py:19
  470.9 188.2 %all-reduce.32.cloned.1.call-start = ((), (), s32[]{:S(2)}) async-start(), calls=%async_computation.7 | async-start | bytes 131072 | tf_op jit(solution)/shard_map/psum | solution.py:19
  581.5 183.6 %all-reduce.34.cloned.1.call-start = ((), (), s32[]{:S(2)}) async-start(), calls=%async_computation.8 | async-start | bytes 262144 | tf_op jit(solution)/shard_map/psum | solution.py:19
  685.9 140.0 %all-reduce.36.cloned.1.call-start = ((), (), s32[]{:S(2)}) async-start(), calls=%async_computation.9 | async-start | bytes 131072 | tf_op jit(solution)/shard_map/psum | solution.py:14
  767.0 146.4 %all-reduce.38.cloned.1.call-start = ((), (), s32[]{:S(2)}) async-start(), calls=%async_computation.10 | async-start | bytes 524288 | tf_op jit(solution)/shard_map/psum | solution.py:19
  829.9 144.8 %all-reduce.40.cloned.1.call-start = ((), (), s32[]{:S(2)}) async-start(), calls=%async_computation.11 | async-start | bytes 262144 | tf_op jit(solution)/shard_map/psum | solution.py:14
  915.3 149.6 %all-reduce.42.cloned.1.call-start = ((), (), s32[]{:S(2)}) async-start(), calls=%async_computation.12 | async-start | bytes 1048576 | tf_op jit(solution)/shard_map/psum | solution.py:19
  980.4 146.4 %all-reduce.44.cloned.1.call-start = ((), (), s32[]{:S(2)}) async-start(), calls=%async_computation.13 | async-start | bytes 524288 | tf_op jit(solution)/shard_map/psum | solution.py:14
  1067.0 155.5 %all-reduce.46.cloned.1.call-start = ((), (), s32[]{:S(2)}) async-start(), calls=%async_computation.14 | async-start | bytes 2097152 | tf_op jit(solution)/shard_map/psum | solution.py:19
  1127.8 1.0 copy-start.5
  1128.8 7.5 copy-start.4
  1130.3 6.5 copy-start.3
  1130.3 92.2 %copy-start.1 = (f32[16,64,256]{2,1,0:T(8,128)S(1)}, f32[16,64,256]{2,1,0:T(8,128)}, u32[]{:S(2)}) copy-start(f32[16,64,256]{2,1,0:T(8,128)} %all-reduce.18.cloned.1.call-done) | copy-start | bytes 3145732
  1136.2 149.1 %copy-start.6 = (f32[31,64,128]{2,1,0:T(8,128)S(1)}, f32[31,64,128]{2,1,0:T(8,128)}, u32[]{:S(2)}) copy-start(f32[31,64,128]{2,1,0:T(8,128)} %copy-done.5) | copy-start | bytes 3047428
  1136.2 149.1 %all-reduce.48.cloned.1.call-start = ((), (), s32[]{:S(2)}) async-start(), calls=%async_computation.15 | async-start | bytes 1048576 | tf_op jit(solution)/shard_map/psum | solution.py:14
  1286.4 1.0 copy-start.7
Sparse Core Ops, SparseCore 0:
  11.8 89.5 all-reduce.17
  110.7 59.0 all-reduce.19
  173.9 84.3 all-reduce.21
  262.4 58.5 all-reduce.23
  324.9 83.3 all-reduce.25
  411.0 57.9 all-reduce.27
  473.2 81.3 all-reduce.29
  581.6 77.4 all-reduce.31
  686.0 79.0 all-reduce.33
  767.8 58.0 all-reduce.35
  830.0 83.3 all-reduce.37
  916.1 58.4 all-reduce.39
  980.5 84.3 all-reduce.41
  1067.6 59.0 all-reduce.43
  1136.3 86.1 all-reduce.45
  1225.3 59.8 all-reduce.47
where the time goes:
time: 1300 us; the launch traced here: 1290 us
  waiting for transfers between devices  1160 us (89%)
  matrix products  51.5 us (4%)
  blocking collectives  48.1 us (4%)
  between operations  14.3 us (1%)
    psum x9, waiting for transfers between devices, sum_rows(): result = lax.psum(values, 'prow')  753 us
    psum x7, waiting for transfers between devices, sum_columns(): result = lax.psum(values, 'pcol')  411 us
    psum x2, blocking collectives, sum_columns(): result = lax.psum(values, 'pcol')  48.1 us
  transfers between devices with their start and end apart: 16, of which 16 were waited for; matrix products, arithmetic and copies ran while one was open for 1% of the time, Pallas kernels for 0%

commit v1 on v0

--- a/solution.py
+++ b/solution.py
@@ -4,6 +4,10 @@
 from jax.sharding import PartitionSpec as P
 
 LEV = 5
+
+
+def lift_the_rings(vals):
+    return lax.all_gather(vals, "prow").sum(axis=0)
 
 
 def block_start(tree_depth):
@@ -16,7 +20,7 @@
 
 
 def sum_rows(values):
-    result = lax.psum(values, "prow")
+    result = lift_the_rings(values)
     return lax.optimization_barrier(result)
 
 

time: 1300 us -> 1170 us (0.900)
  waiting for transfers between devices: 1160 us -> 1000 us
  other arithmetic: 5.02 us -> 39.8 us
    psum x9 -> x0, waiting for transfers between devices: 753 us -> none  [sum_rows(): result = lax.psum(values, 'prow')]
    all_gather x0 -> x9, waiting for transfers between devices: none -> 590 us  [lift_the_rings(): return lax.all_gather(vals, 'prow').sum(axis=0)]
    reduce_sum x0 -> x9, other arithmetic: none -> 32.6 us  [lift_the_rings(): return lax.all_gather(vals, 'prow').sum(axis=0)]
where the time goes in v1:
time: 1170 us
  waiting for transfers between devices  1000 us (85%)
  matrix products  50.1 us (4%)
  blocking collectives  48.7 us (4%)
  other arithmetic  39.8 us (3%)
  between operations  14.2 us (1%)
    all_gather x9, waiting for transfers between devices, lift_the_rings(): return lax.all_gather(vals, 'prow').sum(axis=0)  590 us
    psum x7, waiting for transfers between devices, sum_columns(): result = lax.psum(values, 'pcol')  412 us
    psum x2, blocking collectives, sum_columns(): result = lax.psum(values, 'pcol')  48.7 us
    reduce_sum x9, other arithmetic, lift_the_rings(): return lax.all_gather(vals, 'prow').sum(axis=0)  32.6 us
  transfers between devices with their start and end apart: 16, of which 16 were waited for; matrix products, arithmetic and copies ran while one was open for 1% of the time, Pallas kernels for 0%

profile of v1, /device:TPU:0, one launch (start us, length us, event | category | flops | bytes accessed | tf_op | source)
XLA Modules:
  0.0 1165.0 jit_solution(1185959574398235363)
XLA Ops:
  7.2 2.8 fusion.20
  10.5 114.2 %all-gather.19.cloned.1.call-done = f32[256,64,256]{2,1,0:T(8,128)} async-done(((f32[16,64,256]{2,1,0:T(8,128)}), f32[256,64,256]{2,1,0:T(8,128)}) %all-gather.19.cloned.1.call-update) | async-done | bytes 16777232 | tf_op jit(solution)/shard_map/all_gather | solution.py:10
  124.7 7.4 reduce_sum.173
  132.2 1.7 fusion.5
  133.9 1.7 bitcast_reduce_fusion
  135.6 1.7 bitcast_reduce_fusion.1
  137.4 1.7 bitcast_reduce_fusion.2
  140.1 59.5 %all-reduce.9.cloned.1.call-done = f32[8,64,128]{2,1,0:T(8,128)} async-done(((f32[8,64,128]{2,1,0:T(8,128)}), f32[8,64,128]{2,1,0:T(8,128)}) %all-reduce.9.cloned.1.call-update) | async-done | bytes 262160 | tf_op jit(solution)/shard_map/psum | solution.py:18
  199.6 2.3 fusion.31
  202.3 70.2 %all-gather.21.cloned.1.call-done = f32[128,64,256]{2,1,0:T(8,128)} async-done(((f32[8,64,256]{2,1,0:T(8,128)}), f32[128,64,256]{2,1,0:T(8,128)}) %all-gather.21.cloned.1.call-update) | async-done | bytes 8388624 | tf_op jit(solution)/shard_map/all_gather | solution.py:10
  272.5 4.0 reduce_sum.178
  276.6 1.3 bitcast_reduce_fusion.3
  277.9 1.3 bitcast_reduce_fusion.4
  279.4 0.9 copy-done
  281.1 58.9 %all-reduce.11.cloned.1.call-done = f32[4,64,128]{2,1,0:T(8,128)} async-done(((f32[4,64,128]{2,1,0:T(8,128)}), f32[4,64,128]{2,1,0:T(8,128)}) %all-reduce.11.cloned.1.call-update) | async-done | bytes 131088 | tf_op jit(solution)/shard_map/psum | solution.py:18
  340.0 2.0 fusion.45
  342.4 50.9 %all-gather.23.cloned.1.call-done = f32[64,64,256]{2,1,0:T(8,128)} async-done(((f32[4,64,256]{2,1,0:T(8,128)}), f32[64,64,256]{2,1,0:T(8,128)}) %all-gather.23.cloned.1.call-update) | async-done | bytes 4194320 | tf_op jit(solution)/shard_map/all_gather | solution.py:10
  393.3 2.5 reduce_sum.182
  395.8 1.2 bitcast_reduce_fusion.5
  397.7 58.4 %all-reduce.13.cloned.1.call-done = f32[2,64,128]{2,1,0:T(8,128)} async-done(((f32[2,64,128]{2,1,0:T(8,128)}), f32[2,64,128]{2,1,0:T(8,128)}) %all-reduce.13.cloned.1.call-update) | async-done | bytes 65552 | tf_op jit(solution)/shard_map/psum | solution.py:18
  456.1 1.8 fusion.57
  458.0 1.3 fusion.7
  459.3 1.2 fusion.8
  460.5 42.8 %all-gather.25.cloned.1.call-done = f32[32,64,256]{2,1,0:T(8,128)} async-done(((f32[2,64,256]{2,1,0:T(8,128)}), f32[32,64,256]{2,1,0:T(8,128)}) %all-gather.25.cloned.1.call-update) | async-done | bytes 2097168 | tf_op jit(solution)/shard_map/all_gather | solution.py:10
  503.3 1.7 reduce_sum.185
  505.0 1.1 fusion.9
  506.9 24.6 %psum.66 = f32[1,64,128]{2,1,0:T(8,128)S(1)} all-reduce(f32[1,64,128]{2,1,0:T(8,128)S(1)} %fusion.72), channel_id=1, replica_groups=mesh['prow'=16,'pcol'=8] {'pcol'}, use_global_device_ids=true, to_apply=%region_17.0 | all-reduce | flops 8192 | bytes 65536 | tf_op jit(solution)/shard_map/psum | solution.py:18
  531.4 1.6 fusion.61
  533.2 39.8 %all-gather.27.cloned.1.call-done = f32[1024,256]{1,0:T(8,128)} async-done(((f32[64,256]{1,0:T(8,128)}), f32[1024,256]{1,0:T(8,128)}) %all-gather.27.cloned.1.call-update) | async-done | bytes 1048592 | tf_op jit(solution)/shard_map/all_gather | solution.py:10
  572.9 1.3 reduce.29
  574.2 1.0 convolution_bitcast_fusion
  575.2 24.1 %psum.67 = f32[1,64,128]{2,1,0:T(8,128)S(1)} all-reduce(f32[1,64,128]{2,1,0:T(8,128)S(1)} %convolution_bitcast_fusion), channel_id=1, replica_groups=mesh['prow'=16,'pcol'=8] {'pcol'}, use_global_device_ids=true, to_apply=%region_19.0 | all-reduce | flops 8192 | bytes 65536 | tf_op jit(solution)/shard_map/psum | solution.py:18
  600.0 1.7 convolution_multiply_fusion.18
  601.7 42.5 %all-gather.29.cloned.1.call-done = f32[32,64,256]{2,1,0:T(8,128)} async-done(((f32[2,64,256]{2,1,0:T(8,128)}), f32[32,64,256]{2,1,0:T(8,128)}) %all-gather.29.cloned.1.call-update) | async-done | bytes 2097168 | tf_op jit(solution)/shard_map/all_gather | solution.py:10
  644.2 1.7 reduce_sum.189
  646.0 1.7 fusion.55
  647.7 58.1 %all-reduce.15.cloned.1.call-done = f32[2,64,128]{2,1,0:T(8,128)} async-done(((f32[2,64,128]{2,1,0:T(8,128)}), f32[2,64,128]{2,1,0:T(8,128)}) %all-reduce.15.cloned.1.call-update) | async-done | bytes 65552 | tf_op jit(solution)/shard_map/psum | solution.py:18
  705.8 1.6 fusion.87
  707.4 1.1 convolution_multiply_fusion.12
  708.5 1.8 fusion.6
  710.4 50.7 %all-gather.31.cloned.1.call-done = f32[64,64,256]{2,1,0:T(8,128)} async-done(((f32[4,64,256]{2,1,0:T(8,128)}), f32[64,64,256]{2,1,0:T(8,128)}) %all-gather.31.cloned.1.call-update) | async-done | bytes 4194320 | tf_op jit(solution)/shard_map/all_gather | solution.py:10
  761.2 2.5 reduce_sum.190
  763.7 1.8 fusion.43
  765.5 58.9 %all-reduce.17.cloned.1.call-done = f32[4,64,128]{2,1,0:T(8,128)} async-done(((f32[4,64,128]{2,1,0:T(8,128)}), f32[4,64,128]{2,1,0:T(8,128)}) %all-reduce.17.cloned.1.call-update) | async-done | bytes 131088 | tf_op jit(solution)/shard_map/psum | solution.py:18
  824.5 1.7 fusion.86
  826.1 1.3 convolution_multiply_fusion.10
  827.4 1.3 fusion.4
  828.7 2.1 fusion.3
  830.8 70.0 %all-gather.33.cloned.1.call-done = f32[128,64,256]{2,1,0:T(8,128)} async-done(((f32[8,64,256]{2,1,0:T(8,128)}), f32[128,64,256]{2,1,0:T(8,128)}) %all-gather.33.cloned.1.call-update) | async-done | bytes 8388624 | tf_op jit(solution)/shard_map/all_gather | solution.py:10
  900.8 4.0 reduce_sum.191
  904.8 2.0 fusion.29
  906.9 59.5 %all-reduce.19.cloned.1.call-done = f32[8,64,128]{2,1,0:T(8,128)} async-done(((f32[8,64,128]{2,1,0:T(8,128)}), f32[8,64,128]{2,1,0:T(8,128)}) %all-reduce.19.cloned.1.call-update) | async-done | bytes 262160 | tf_op jit(solution)/shard_map/psum | solution.py:18
  966.4 1.8 fusion.85
  968.3 1.5 convolution_multiply_fusion.3
  969.8 1.5 fusion.2
  971.4 1.5 fusion.1
  973.0 2.5 fusion
  977.6 108.7 %all-gather.35.cloned.1.call-done = f32[256,64,256]{2,1,0:T(8,128)} async-done(((f32[16,64,256]{2,1,0:T(8,128)}), f32[256,64,256]{2,1,0:T(8,128)}) %all-gather.35.cloned.1.call-update) | async-done | bytes 16777232 | tf_op jit(solution)/shard_map/all_gather | solution.py:10
  1086.3 7.4 reduce_sum.192
  1093.7 2.4 fusion.18
  1096.1 0.8 constant_dynamic-update-slice_fusion.6
  1096.9 1.1 constant_dynamic-update-slice_fusion.5
  1098.0 58.6 %all-reduce.21.cloned.1.call-done = f32[16,64,128]{2,1,0:T(8,128)} async-done(((f32[16,64,128]{2,1,0:T(8,128)}), f32[16,64,128]{2,1,0:T(8,128)}) %all-reduce.21.cloned.1.call-update) | async-done | bytes 524304 | tf_op jit(solution)/shard_map/psum | solution.py:18
  1156.6 1.9 constant_dynamic-update-slice_fusion
  (67 shorter events, 8.0 us)
Async XLA Ops:
  7.2 3.0 copy-start.1
  7.2 117.5 %all-gather.19.cloned.1.call-start = ((), (), s32[]{:S(2)}) async-start(), calls=%async_computation.7 | async-start | bytes 17825792 | tf_op jit(solution)/shard_map/all_gather | solution.py:10
  10.1 189.5 %all-reduce.9.cloned.1.call-start = ((), (), s32[]{:S(2)}) async-start(), calls=%async_computation | async-start | bytes 524288 | tf_op jit(solution)/shard_map/psum | solution.py:18
  140.0 132.5 %all-gather.21.cloned.1.call-start = ((), (), s32[]{:S(2)}) async-start(), calls=%async_computation.8 | async-start | bytes 8912896 | tf_op jit(solution)/shard_map/all_gather | solution.py:10
  201.9 138.1 %all-reduce.11.cloned.1.call-start = ((), (), s32[]{:S(2)}) async-start(), calls=%async_computation.1 | async-start | bytes 262144 | tf_op jit(solution)/shard_map/psum | solution.py:18
  279.4 1.0 copy-start
  281.0 112.3 %all-gather.23.cloned.1.call-start = ((), (), s32[]{:S(2)}) async-start(), calls=%async_computation.9 | async-start | bytes 4456448 | tf_op jit(solution)/shard_map/all_gather | solution.py:10
  342.0 114.1 %all-reduce.13.cloned.1.call-start = ((), (), s32[]{:S(2)}) async-start(), calls=%async_computation.2 | async-start | bytes 131072 | tf_op jit(solution)/shard_map/psum | solution.py:18
  397.6 105.7 %all-gather.25.cloned.1.call-start = ((), (), s32[]{:S(2)}) async-start(), calls=%async_computation.10 | async-start | bytes 2228224 | tf_op jit(solution)/shard_map/all_gather | solution.py:10
  457.9 115.0 %all-gather.27.cloned.1.call-start = ((), (), s32[]{:S(2)}) async-start(), calls=%async_computation.11 | async-start | bytes 1114112 | tf_op jit(solution)/shard_map/all_gather | solution.py:10
  533.1 111.1 %all-gather.29.cloned.1.call-start = ((), (), s32[]{:S(2)}) async-start(), calls=%async_computation.12 | async-start | bytes 2228224 | tf_op jit(solution)/shard_map/all_gather | solution.py:10
  601.7 104.1 %all-reduce.15.cloned.1.call-start = ((), (), s32[]{:S(2)}) async-start(), calls=%async_computation.3 | async-start | bytes 131072 | tf_op jit(solution)/shard_map/psum | solution.py:18
  647.7 113.5 %all-gather.31.cloned.1.call-start = ((), (), s32[]{:S(2)}) async-start(), calls=%async_computation.13 | async-start | bytes 4456448 | tf_op jit(solution)/shard_map/all_gather | solution.py:10
  710.4 114.1 %all-reduce.17.cloned.1.call-start = ((), (), s32[]{:S(2)}) async-start(), calls=%async_computation.4 | async-start | bytes 262144 | tf_op jit(solution)/shard_map/psum | solution.py:18
  765.5 135.3 %all-gather.33.cloned.1.call-start = ((), (), s32[]{:S(2)}) async-start(), calls=%async_computation.14 | async-start | bytes 8912896 | tf_op jit(solution)/shard_map/all_gather | solution.py:10
  830.8 135.6 %all-reduce.19.cloned.1.call-start = ((), (), s32[]{:S(2)}) async-start(), calls=%async_computation.5 | async-start | bytes 524288 | tf_op jit(solution)/shard_map/psum | solution.py:18
  906.8 179.4 %all-gather.35.cloned.1.call-start = ((), (), s32[]{:S(2)}) async-start(), calls=%async_computation.15 | async-start | bytes 17825792 | tf_op jit(solution)/shard_map/all_gather | solution.py:10
  975.5 181.1 %all-reduce.21.cloned.1.call-start = ((), (), s32[]{:S(2)}) async-start(), calls=%async_computation.6 | async-start | bytes 1048576 | tf_op jit(solution)/shard_map/psum | solution.py:18
Sparse Core Ops, SparseCore 0:
  10.7 113.9 all-gather.18
  140.1 59.4 all-reduce.8
  202.5 69.9 all-gather.20
  281.2 58.7 all-reduce.10
  342.6 50.6 all-gather.22
  397.8 58.2 all-reduce.12
  459.0 44.2 all-gather.24
  533.2 39.6 all-gather.26
  601.8 42.3 all-gather.28
  647.8 57.9 all-reduce.14
  710.5 50.6 all-gather.30
  765.6 58.7 all-reduce.16
  830.9 69.8 all-gather.32
  907.0 59.4 all-reduce.18
  975.7 110.5 all-gather.34
  1096.2 60.3 all-reduce.20
